TPU v7x, 512 devices: a whole 4x8x8 slice. The times are simulated.
512 devices in a mesh: tm: 32 (over y, x), chan: 16 (over z, core).
Axes of the slice: x: 4, y: 8, z: 8, core: 2. Of those that a mesh axis runs over, the one named last changes fastest.
Arguments:
- record: bfloat16 [32768, 10240], P('tm', 'chan'), may hold values from -6 to 6
- fir_taps: bfloat16 [64], replicated, may hold values from -0.75 to 0.75
- gauge_lag: int32 [10240], P('chan'), may hold values from 1 to 16
- projector: bfloat16 [32768, 128], P('tm'), may hold values from -0.1875 to 0.1875
- compress: float32 [256, 128], replicated, may hold values from -0.5 to 0.5
Outputs:
- sketch: float32 [128, 10240], P('tm', 'chan')
Inputs may be any that keep to these rules, and one draw needn't show every extreme that they name: `gauge_lag`: some channel has lag 16.
All inputs are finite; a program needn't handle non-finite values.
Results may differ from a plain program's by a relative error of at most 0.0028.
Values may be sent and summed in bfloat16 or wider, within the bound.
A program may use at most 64 MiB of HBM per device.

v0:
```python
import jax
import jax.numpy as jnp
from jax import lax
from jax.sharding import PartitionSpec as P

TAPS = 64
GAUGE_MAX = 16
K_ITERS = 8


def from_behind(value, axis, steps):
    count = lax.axis_size(axis)
    first, last = (max(0, -steps), min(count, count - steps))
    return lax.ppermute(value, axis, [(source, source + steps) for source in range(first, last)])


def from_partner(value, axis, bit):
    mask = 2**bit
    pairs = [(source, source ^ mask) for source in range(lax.axis_size(axis))]
    return lax.ppermute(value, axis, pairs)


def toeplitz_block(fir_taps, out_count):
    row_ids = jnp.arange(out_count, dtype=jnp.int32)[:, None]
    col_ids = jnp.arange(out_count + TAPS - 1, dtype=jnp.int32)[None, :]
    offset = row_ids + TAPS - 1 - col_ids
    tap_ids = jnp.arange(TAPS, dtype=jnp.int32)
    onehot = (offset[:, :, None] == tap_ids[None, None, :]).astype(jnp.float32)
    return jnp.sum(onehot * fir_taps.astype(jnp.float32)[None, None, :], axis=2).astype(
        jnp.bfloat16
    )


def filter_mix(gram, compress):
    width = gram.shape[0]
    eye = jnp.eye(width, dtype=jnp.float32)
    mean_level = jnp.trace(gram) / width
    shifted = gram - mean_level * eye
    signed = shifted / jnp.sqrt(jnp.sum(shifted * shifted) + 1e-06)
    for step_index in range(K_ITERS):
        square = jnp.dot(
            signed, signed, precision=lax.Precision.HIGHEST, preferred_element_type=jnp.float32
        )
        signed = jnp.dot(
            signed,
            1.5 * eye - 0.5 * square,
            precision=lax.Precision.HIGHEST,
            preferred_element_type=jnp.float32,
        )
    filter_mat = 0.5 * (eye + signed)
    return jnp.dot(
        compress.T, filter_mat, precision=lax.Precision.HIGHEST, preferred_element_type=jnp.float32
    )


def inner_rows(first_mat, second_mat):
    return jnp.dot(
        first_mat, second_mat.T, precision=lax.Precision.HIGHEST, preferred_element_type=jnp.float32
    )


def on_device(record, fir_taps, gauge_lag, projector, compress):
    sample_rows = record.shape[0]
    column_count = record.shape[1]
    halo_rows = TAPS - 1 + GAUGE_MAX
    tail_rows = record[sample_rows - halo_rows :]
    before = from_behind(tail_rows, "tm", 1)
    extended = jnp.concatenate([before, record], 0)
    lead_matrix = toeplitz_block(fir_taps, GAUGE_MAX)
    lead_part = jnp.dot(
        lead_matrix, extended[: GAUGE_MAX + TAPS - 1], preferred_element_type=jnp.float32
    )
    block_rows = min(128, sample_rows)
    main_matrix = toeplitz_block(fir_taps, block_rows)

    def filter_block(block_index):
        segment = lax.dynamic_slice_in_dim(
            extended, GAUGE_MAX + block_index * block_rows, block_rows + TAPS - 1, 0
        )
        return jnp.dot(main_matrix, segment, preferred_element_type=jnp.float32)

    main_part = lax.map(filter_block, jnp.arange(sample_rows // block_rows, dtype=jnp.int32))
    filtered = jnp.concatenate([lead_part, main_part.reshape(sample_rows, column_count)], 0)
    current = filtered[GAUGE_MAX:]
    lagged = jnp.zeros((sample_rows, column_count), jnp.float32)
    for lag_step in range(1, GAUGE_MAX + 1):
        chosen = (gauge_lag == lag_step).astype(jnp.float32)[None, :]
        lagged = (
            lagged + chosen * filtered[GAUGE_MAX - lag_step : GAUGE_MAX - lag_step + sample_rows]
        )
    strain = (current - lagged).astype(jnp.bfloat16)
    sketch = lax.dot_general(
        projector, strain, (((0,), (0,)), ((), ())), preferred_element_type=jnp.float32
    )
    depth_count = lax.axis_size("tm").bit_length() - 1
    position = lax.axis_index("tm")
    for depth_level in range(depth_count):
        is_lower = position // 2**depth_level % 2 == 0
        partner = from_partner(sketch, "tm", depth_level)
        stacked = jnp.where(
            is_lower, jnp.concatenate([sketch, partner], 0), jnp.concatenate([partner, sketch], 0)
        )
        gram = lax.psum(inner_rows(stacked, stacked), "chan")
        mixing = filter_mix(gram, compress)
        sketch = jnp.dot(
            mixing, stacked, precision=lax.Precision.HIGHEST, preferred_element_type=jnp.float32
        )
    share_rows = sketch.shape[0] // lax.axis_size("tm")
    return lax.dynamic_slice_in_dim(sketch, position * share_rows, share_rows, 0)


def solution(mesh):
    return jax.shard_map(
        on_device,
        mesh=mesh,
        in_specs=(P("tm", "chan"), P(), P("chan"), P("tm", None), P()),
        out_specs=P("tm", "chan"),
        check_vma=False,
    )
```

profile of v0, /device:TPU:1, one launch (start us, length us, event | category | flops | bytes accessed | tf_op | source)
XLA Modules:
  0.0 803.2 jit_solution(263706194352711852)
XLA Ops:
  6.5 1.0 slice.51
  7.5 3.9 collective-permute-start
  11.5 0.7 convert_element_type.79
  12.2 2.0 select_reduce_fusion
  14.4 0.7 compare_convert_fusion.15
  15.2 1.6 pad_maximum_fusion.1
  16.9 19.6 %while.12 = (s32[]{:T(128)}, f32[8,128,640]{2,1,0:T(8,128)}, s32[8]{0:T(128)S(1)}, bf16[1103,640]{1,0:T(8,128)(2,1)S(1)}, bf16[128,191]{1,0:T(8,128)(2,1)S(1)}, ...) while((s32[]{:T(128)}, f32[8,128,640]{2,1,0:T(8,128)}, s32[8]{0:T(128)S(1)}, ...), condition=%wide.region_2.3_spmd, body=%wide.region_1.0_spmd.sunk | while | flops 31293448 | bytes 1949883 | solution.py:82
  16.9 0.6 dynamic_slice.23
  18.6 0.7 constant_dynamic-update-slice_fusion.2
  19.3 0.6 dynamic_slice.23
  21.0 0.8 constant_dynamic-update-slice_fusion.2
  23.5 0.8 constant_dynamic-update-slice_fusion.2
  25.9 0.8 constant_dynamic-update-slice_fusion.2
  28.4 0.8 constant_dynamic-update-slice_fusion.2
  30.9 0.7 constant_dynamic-update-slice_fusion.2
  33.3 0.8 constant_dynamic-update-slice_fusion.2
  35.8 0.7 constant_dynamic-update-slice_fusion.2
  36.6 24.8 %fusion.52 = f32[128,640]{1,0:T(8,128)S(1)} fusion(bf16[1024,128]{1,0:T(8,128)(2,1)S(1)} %copy-done, f32[1024,640]{1,0:T(8,128)} %bitcast.181, f32[16,640]{1,0:T(8,128)S(1)} %fusion.158, f32[640]{0:T(1024)S(1)} %get-tuple-element.100, f32[640]{0:T(1024)S(1)} %get-tuple-element.101, f32[640]{0:T(1024)S(1)} %get-tuple-element.87, ...), kind=kOutput, calls=%fused_computation.121 | convolution fusion | flops 199884800 | bytes 3293184 | tf_op jit(solution)/shard_map/dot_general | solution.py:92
  61.4 3.1 collective-permute-start.1
  64.6 4.7 collective-permute-done.1
  69.3 1.5 fusion.69
  71.4 123.7 %all-reduce.6.cloned.1.call-done = f32[256,256]{1,0:T(8,128)} async-done(((f32[256,256]{1,0:T(8,128)}), f32[256,256]{1,0:T(8,128)}) %all-reduce.6.cloned.1.call-update) | async-done | bytes 262160 | tf_op jit(solution)/shard_map/psum | solution.py:103
  195.1 1.6 select_reduce_fusion.6
  197.4 1.6 multiply_reduce_fusion.4
  199.7 1.5 select_subtract_fusion.39
  201.1 1.4 fusion.97
  207.9 0.6 fusion.129
  209.1 4.6 collective-permute-start.2
  213.8 7.4 collective-permute-done.2
  221.2 1.5 fusion.67
  223.0 115.3 %all-reduce.8.cloned.1.call-done = f32[256,256]{1,0:T(8,128)} async-done(((f32[256,256]{1,0:T(8,128)}), f32[256,256]{1,0:T(8,128)}) %all-reduce.8.cloned.1.call-update) | async-done | bytes 262160 | tf_op jit(solution)/shard_map/psum | solution.py:103
  338.3 1.6 select_reduce_fusion.5
  340.5 1.6 multiply_reduce_fusion.3
  342.8 1.5 select_subtract_fusion.31
  344.3 1.3 fusion.94
  351.1 0.6 fusion.136
  352.3 3.1 collective-permute-start.3
  355.4 7.4 collective-permute-done.3
  362.8 1.5 fusion.65
  364.6 115.3 %all-reduce.10.cloned.1.call-done = f32[256,256]{1,0:T(8,128)} async-done(((f32[256,256]{1,0:T(8,128)}), f32[256,256]{1,0:T(8,128)}) %all-reduce.10.cloned.1.call-update) | async-done | bytes 262160 | tf_op jit(solution)/shard_map/psum | solution.py:103
  479.9 1.6 select_reduce_fusion.4
  482.2 1.6 multiply_reduce_fusion.2
  484.5 1.5 select_subtract_fusion.23
  486.0 1.4 fusion.91
  492.7 0.6 fusion.143
  493.9 4.0 collective-permute-start.4
  498.0 14.5 %collective-permute-done.4 = f32[128,640]{1,0:T(8,128)S(1)} collective-permute-done((f32[128,640]{1,0:T(8,128)S(1)}, f32[128,640]{1,0:T(8,128)S(1)}, u32[]{:S(2)}, u32[]{:S(2)}) %collective-permute-start.4) | collective-permute-done | bytes 327712 | tf_op jit(solution)/shard_map/ppermute | solution.py:20
  512.5 1.5 fusion.63
  514.3 115.4 %all-reduce.12.cloned.1.call-done = f32[256,256]{1,0:T(8,128)} async-done(((f32[256,256]{1,0:T(8,128)}), f32[256,256]{1,0:T(8,128)}) %all-reduce.12.cloned.1.call-update) | async-done | bytes 262160 | tf_op jit(solution)/shard_map/psum | solution.py:103
  629.7 1.6 select_reduce_fusion.3
  631.9 1.6 multiply_reduce_fusion.1
  634.3 1.4 select_subtract_fusion.15
  635.7 1.3 fusion.88
  642.5 0.6 fusion.150
  643.7 7.4 collective-permute-start.5
  651.1 8.9 %collective-permute-done.5 = f32[128,640]{1,0:T(8,128)S(1)} collective-permute-done((f32[128,640]{1,0:T(8,128)S(1)}, f32[128,640]{1,0:T(8,128)S(1)}, u32[]{:S(2)}, u32[]{:S(2)}) %collective-permute-start.5) | collective-permute-done | bytes 327712 | tf_op jit(solution)/shard_map/ppermute | solution.py:20
  660.0 1.5 fusion.61
  661.6 120.0 %all-reduce.14.cloned.1.call-done = f32[256,256]{1,0:T(8,128)} async-done(((f32[256,256]{1,0:T(8,128)}), f32[256,256]{1,0:T(8,128)}) %all-reduce.14.cloned.1.call-update) | async-done | bytes 262160 | tf_op jit(solution)/shard_map/psum | solution.py:103
  781.6 1.6 select_reduce_fusion.2
  783.8 1.6 multiply_reduce_fusion
  786.1 1.5 select_subtract_fusion.7
  787.6 1.3 fusion.85
  794.4 0.6 fusion.157
  795.6 0.6 constant_dynamic-slice_fusion
  (121 shorter events, 38.7 us)
Async XLA Ops:
  6.5 30.1 %copy-start = (bf16[1024,128]{1,0:T(8,128)(2,1)S(1)}, bf16[1024,128]{1,0:T(8,128)(2,1)}, u32[]{:S(2)}) copy-start(bf16[1024,128]{1,0:T(8,128)(2,1)} %param.10) | copy-start | bytes 786436
  6.5 188.6 %all-reduce.6.cloned.1.call-start = ((), (), s32[]{:S(2)}) async-start(), calls=%async_computation | async-start | bytes 524288 | tf_op jit(solution)/shard_map/psum | solution.py:103
  7.5 7.7 collective-permute-start
  61.4 7.8 collective-permute-start.1
  70.8 267.5 %all-reduce.8.cloned.1.call-start = ((), (), s32[]{:S(2)}) async-start(), calls=%async_computation.1 | async-start | bytes 524288 | tf_op jit(solution)/shard_map/psum | solution.py:103
  205.2 2.7 copy-start.1
  209.1 12.1 %collective-permute-start.2 = (f32[128,640]{1,0:T(8,128)S(1)}, f32[128,640]{1,0:T(8,128)S(1)}, u32[]{:S(2)}, u32[]{:S(2)}) collective-permute-start(f32[128,640]{1,0:T(8,128)S(1)} %fusion.68), channel_id=1, source_target_pairs={{0,32},{16,48},{32,0},{48,16},{64,96},{80,112},{96,64},{112,80},{1... | collective-permute-start | bytes 983048 | tf_op jit(solution)/shard_map/ppermute | solution.py:20
  222.7 257.2 %all-reduce.10.cloned.1.call-start = ((), (), s32[]{:S(2)}) async-start(), calls=%async_computation.2 | async-start | bytes 524288 | tf_op jit(solution)/shard_map/psum | solution.py:103
  352.3 10.5 %collective-permute-start.3 = (f32[128,640]{1,0:T(8,128)S(1)}, f32[128,640]{1,0:T(8,128)S(1)}, u32[]{:S(2)}, u32[]{:S(2)}) collective-permute-start(f32[128,640]{1,0:T(8,128)S(1)} %fusion.66), channel_id=1, source_target_pairs={{0,64},{16,80},{32,96},{48,112},{64,0},{80,16},{96,32},{112,48},{1... | collective-permute-start | bytes 983048 | tf_op jit(solution)/shard_map/ppermute | solution.py:20
  364.4 265.3 %all-reduce.12.cloned.1.call-start = ((), (), s32[]{:S(2)}) async-start(), calls=%async_computation.3 | async-start | bytes 524288 | tf_op jit(solution)/shard_map/psum | solution.py:103
  493.9 18.5 %collective-permute-start.4 = (f32[128,640]{1,0:T(8,128)S(1)}, f32[128,640]{1,0:T(8,128)S(1)}, u32[]{:S(2)}, u32[]{:S(2)}) collective-permute-start(f32[128,640]{1,0:T(8,128)S(1)} %fusion.64), channel_id=1, source_target_pairs={{0,128},{16,144},{32,160},{48,176},{64,192},{80,208},{96,224},{112... | collective-permute-start | bytes 983048 | tf_op jit(solution)/shard_map/ppermute | solution.py:20
  514.0 267.6 %all-reduce.14.cloned.1.call-start = ((), (), s32[]{:S(2)}) async-start(), calls=%async_computation.4 | async-start | bytes 524288 | tf_op jit(solution)/shard_map/psum | solution.py:103
  643.7 16.3 %collective-permute-start.5 = (f32[128,640]{1,0:T(8,128)S(1)}, f32[128,640]{1,0:T(8,128)S(1)}, u32[]{:S(2)}, u32[]{:S(2)}) collective-permute-start(f32[128,640]{1,0:T(8,128)S(1)} %fusion.62), channel_id=1, source_target_pairs={{0,256},{16,272},{32,288},{48,304},{64,320},{80,336},{96,352},{112... | collective-permute-start | bytes 983048 | tf_op jit(solution)/shard_map/ppermute | solution.py:20
Sparse Core Ops, SparseCore 0:
  70.9 124.1 all-reduce.5
  222.9 115.3 all-reduce.7
  364.5 115.3 all-reduce.9
  514.1 115.5 all-reduce.11
  661.7 119.8 all-reduce.13
where the time goes:
time: 809 us; the launch traced here: 803 us
  waiting for transfers between devices  633 us (78%)
  matrix products  81.5 us (10%)
  starting transfers between devices  27.5 us (3%)
  other arithmetic  21.4 us (3%)
  between operations  21.3 us (3%)
  local copies, waits for them, and re-layouts  13.8 us (2%)
    psum x5, waiting for transfers between devices, on_device(): gram = lax.psum(inner_rows(stacked, stacked), 'chan')  590 us
    ppermute x5, waiting for transfers between devices, from_partner(): return lax.ppermute(value, axis, pairs)  42.9 us
    dot_general x1, matrix products, on_device(): lax.dot_general(projector, strain, (((0,), (0,)), ((), ())), preferred_el...  24.8 us
    ppermute x5, starting transfers between devices, from_partner(): return lax.ppermute(value, axis, pairs)  22.3 us
    dot_general x40, matrix products, filter_mix(): jnp.dot(signed, signed, precision=lax.Precision.HIGHEST, preferred_elemen...  20.5 us
    dot_general x40, matrix products, filter_mix(): jnp.dot(signed, 1.5 * eye - 0.5 * square, precision=lax.Precision.HIGHEST...  20 us
  transfers between devices with their start and end apart: 11, of which 10 were waited for; matrix products, arithmetic and copies ran while one was open for 0% of the time, Pallas kernels for 0%

commit v1 on v0

--- a/solution.py
+++ b/solution.py
@@ -100,7 +100,9 @@
         stacked = jnp.where(
             is_lower, jnp.concatenate([sketch, partner], 0), jnp.concatenate([partner, sketch], 0)
         )
-        gram = lax.psum(inner_rows(stacked, stacked), "chan")
+        own = inner_rows(stacked, stacked)
+        pieces = lax.all_gather(own, "chan", axis=0, tiled=False)
+        gram = pieces.sum(axis=0)
         mixing = filter_mix(gram, compress)
         sketch = jnp.dot(
             mixing, stacked, precision=lax.Precision.HIGHEST, preferred_element_type=jnp.float32

time: 809 us -> 446 us (0.55)
  waiting for transfers between devices: 633 us -> 278 us
  matrix products: 81.5 us -> 71.4 us
    psum x5 -> x0, waiting for transfers between devices: 590 us -> none  [on_device(): gram = lax.psum(inner_rows(stacked, stacked), 'chan')]
    all_gather x0 -> x5, waiting for transfers between devices: none -> 231 us  [on_device(): pieces = lax.all_gather(own, 'chan', axis=0, tiled=False)]
    reduce_sum x0 -> x5, other arithmetic: none -> 12.4 us  [on_device(): gram = pieces.sum(axis=0)]
  transfers between devices with their start and end apart: 11 -> 11, of which waited for: 10 -> 10; matrix products, arithmetic and copies ran while one was open for 0% -> 1% of each run, Pallas kernels for 0% -> 0%
where the time goes in v1:
time: 446 us; the launch traced here: 441 us
  waiting for transfers between devices  278 us (62%)
  matrix products  71.4 us (16%)
  starting transfers between devices  27 us (6%)
  other arithmetic  24.2 us (5%)
  between operations  21.3 us (5%)
  local copies, waits for them, and re-layouts  13.8 us (3%)
  loops' own time  5.11 us (1%)
    all_gather x5, waiting for transfers between devices, on_device(): pieces = lax.all_gather(own, 'chan', axis=0, tiled=False)  231 us
    ppermute x5, waiting for transfers between devices, from_partner(): return lax.ppermute(value, axis, pairs)  46.7 us
    dot_general x1, matrix products, on_device(): lax.dot_general(projector, strain, (((0,), (0,)), ((), ())), preferred_el...  24.8 us
    ppermute x5, starting transfers between devices, from_partner(): return lax.ppermute(value, axis, pairs)  21.7 us
    dot_general x40, matrix products, filter_mix(): jnp.dot(signed, signed, precision=lax.Precision.HIGHEST, preferred_elemen...  15.3 us
    dot_general x40, matrix products, filter_mix(): jnp.dot(signed, 1.5 * eye - 0.5 * square, precision=lax.Precision.HIGHEST...  15.2 us
    reduce_sum x5, other arithmetic, on_device(): gram = pieces.sum(axis=0)  12.4 us
  transfers between devices with their start and end apart: 11, of which 10 were waited for; matrix products, arithmetic and copies ran while one was open for 1% of the time, Pallas kernels for 0%

profile of v1, /device:TPU:1, one launch (start us, length us, event | category | flops | bytes accessed | tf_op | source)
XLA Modules:
  0.0 440.9 jit_solution(13508083316437326486)
XLA Ops:
  6.5 1.0 slice.51
  7.5 3.9 collective-permute-start
  11.5 0.7 convert_element_type.79
  12.2 2.0 select_reduce_fusion
  14.4 0.7 compare_convert_fusion.15
  15.3 1.6 pad_maximum_fusion.1
  16.9 19.6 %while.12 = (s32[]{:T(128)}, f32[8,128,640]{2,1,0:T(8,128)}, s32[8]{0:T(128)S(1)}, bf16[1103,640]{1,0:T(8,128)(2,1)S(1)}, bf16[128,191]{1,0:T(8,128)(2,1)S(1)}, ...) while((s32[]{:T(128)}, f32[8,128,640]{2,1,0:T(8,128)}, s32[8]{0:T(128)S(1)}, ...), condition=%wide.region_2.3_spmd, body=%wide.region_1.0_spmd.sunk | while | flops 31293448 | bytes 1949883 | solution.py:82
  16.9 0.6 dynamic_slice.23
  18.6 0.7 constant_dynamic-update-slice_fusion.2
  19.4 0.6 dynamic_slice.23
  21.1 0.8 constant_dynamic-update-slice_fusion.2
  21.8 0.6 dynamic_slice.23
  23.5 0.8 constant_dynamic-update-slice_fusion.2
  24.3 0.6 dynamic_slice.23
  26.0 0.8 constant_dynamic-update-slice_fusion.2
  26.7 0.6 dynamic_slice.23
  28.4 0.8 constant_dynamic-update-slice_fusion.2
  29.2 0.6 dynamic_slice.23
  30.9 0.7 constant_dynamic-update-slice_fusion.2
  31.6 0.6 dynamic_slice.23
  33.3 0.8 constant_dynamic-update-slice_fusion.2
  35.8 0.7 constant_dynamic-update-slice_fusion.2
  36.7 24.8 %fusion.52 = f32[128,640]{1,0:T(8,128)S(1)} fusion(bf16[1024,128]{1,0:T(8,128)(2,1)S(1)} %copy-done, f32[1024,640]{1,0:T(8,128)} %bitcast.191, f32[16,640]{1,0:T(8,128)S(1)} %fusion.158, f32[640]{0:T(1024)S(1)} %get-tuple-element.100, f32[640]{0:T(1024)S(1)} %get-tuple-element.101, f32[640]{0:T(1024)S(1)} %get-tuple-element.87, ...), kind=kOutput, calls=%fused_computation.121 | convolution fusion | flops 199884800 | bytes 3293184 | tf_op jit(solution)/shard_map/dot_general | solution.py:92
  61.4 3.1 collective-permute-start.1
  64.6 4.7 %collective-permute-done.1 = f32[128,640]{1,0:T(8,128)S(1)} collective-permute-done((f32[128,640]{1,0:T(8,128)S(1)}, f32[128,640]{1,0:T(8,128)S(1)}, u32[]{:S(2)}, u32[]{:S(2)}) %collective-permute-start.1) | collective-permute-done | bytes 327712 | tf_op jit(solution)/shard_map/ppermute | solution.py:20
  69.3 1.5 fusion.69
  71.4 53.0 %all-gather.11.cloned.1.call-done = f32[4096,256]{1,0:T(8,128)} async-done(((f32[256,256]{1,0:T(8,128)}), f32[4096,256]{1,0:T(8,128)}) %all-gather.11.cloned.1.call-update) | async-done | bytes 4194320 | tf_op jit(solution)/shard_map/all_gather | solution.py:104
  124.4 2.5 reduce_sum.144
  126.9 0.6 select_reduce_fusion.6
  128.2 0.7 multiply_reduce_fusion.4
  135.8 0.6 fusion.129
  137.0 4.4 %collective-permute-start.2 = (f32[128,640]{1,0:T(8,128)S(1)}, f32[128,640]{1,0:T(8,128)S(1)}, u32[]{:S(2)}, u32[]{:S(2)}) collective-permute-start(f32[128,640]{1,0:T(8,128)S(1)} %fusion.68), channel_id=1, source_target_pairs={{0,32},{16,48},{32,0},{48,16},{64,96},{80,112},{96,64},{112,80},{1... | collective-permute-start | bytes 983048 | tf_op jit(solution)/shard_map/ppermute | solution.py:20
  141.4 7.9 %collective-permute-done.2 = f32[128,640]{1,0:T(8,128)S(1)} collective-permute-done((f32[128,640]{1,0:T(8,128)S(1)}, f32[128,640]{1,0:T(8,128)S(1)}, u32[]{:S(2)}, u32[]{:S(2)}) %collective-permute-start.2) | collective-permute-done | bytes 327712 | tf_op jit(solution)/shard_map/ppermute | solution.py:20
  149.4 1.5 fusion.67
  151.1 44.0 %all-gather.13.cloned.1.call-done = f32[4096,256]{1,0:T(8,128)} async-done(((f32[256,256]{1,0:T(8,128)}), f32[4096,256]{1,0:T(8,128)}) %all-gather.13.cloned.1.call-update) | async-done | bytes 4194320 | tf_op jit(solution)/shard_map/all_gather | solution.py:104
  195.1 2.5 reduce_sum.147
  197.6 0.6 select_reduce_fusion.5
  198.9 0.7 multiply_reduce_fusion.3
  206.5 0.6 fusion.136
  207.7 2.9 collective-permute-start.3
  210.7 7.9 %collective-permute-done.3 = f32[128,640]{1,0:T(8,128)S(1)} collective-permute-done((f32[128,640]{1,0:T(8,128)S(1)}, f32[128,640]{1,0:T(8,128)S(1)}, u32[]{:S(2)}, u32[]{:S(2)}) %collective-permute-start.3) | collective-permute-done | bytes 327712 | tf_op jit(solution)/shard_map/ppermute | solution.py:20
  218.6 1.5 fusion.65
  220.4 44.0 %all-gather.15.cloned.1.call-done = f32[4096,256]{1,0:T(8,128)} async-done(((f32[256,256]{1,0:T(8,128)}), f32[4096,256]{1,0:T(8,128)}) %all-gather.15.cloned.1.call-update) | async-done | bytes 4194320 | tf_op jit(solution)/shard_map/all_gather | solution.py:104
  264.3 2.5 reduce_sum.150
  266.8 0.6 select_reduce_fusion.4
  268.1 0.7 multiply_reduce_fusion.2
  275.7 0.6 fusion.143
  276.9 4.0 collective-permute-start.4
  281.0 14.7 %collective-permute-done.4 = f32[128,640]{1,0:T(8,128)S(1)} collective-permute-done((f32[128,640]{1,0:T(8,128)S(1)}, f32[128,640]{1,0:T(8,128)S(1)}, u32[]{:S(2)}, u32[]{:S(2)}) %collective-permute-start.4) | collective-permute-done | bytes 327712 | tf_op jit(solution)/shard_map/ppermute | solution.py:20
  295.7 1.5 fusion.63
  297.6 43.9 %all-gather.17.cloned.1.call-done = f32[4096,256]{1,0:T(8,128)} async-done(((f32[256,256]{1,0:T(8,128)}), f32[4096,256]{1,0:T(8,128)}) %all-gather.17.cloned.1.call-update) | async-done | bytes 4194320 | tf_op jit(solution)/shard_map/all_gather | solution.py:104
  341.5 2.5 reduce_sum.153
  344.0 0.6 select_reduce_fusion.3
  345.2 0.7 multiply_reduce_fusion.1
  352.8 0.6 fusion.150
  354.0 7.2 %collective-permute-start.5 = (f32[128,640]{1,0:T(8,128)S(1)}, f32[128,640]{1,0:T(8,128)S(1)}, u32[]{:S(2)}, u32[]{:S(2)}) collective-permute-start(f32[128,640]{1,0:T(8,128)S(1)} %fusion.62), channel_id=1, source_target_pairs={{0,256},{16,272},{32,288},{48,304},{64,320},{80,336},{96,352},{112... | collective-permute-start | bytes 983048 | tf_op jit(solution)/shard_map/ppermute | solution.py:20
  361.3 11.4 %collective-permute-done.5 = f32[128,640]{1,0:T(8,128)S(1)} collective-permute-done((f32[128,640]{1,0:T(8,128)S(1)}, f32[128,640]{1,0:T(8,128)S(1)}, u32[]{:S(2)}, u32[]{:S(2)}) %collective-permute-start.5) | collective-permute-done | bytes 327712 | tf_op jit(solution)/shard_map/ppermute | solution.py:20
  372.7 1.5 fusion.61
  374.2 46.5 %all-gather.19.cloned.1.call-done = f32[4096,256]{1,0:T(8,128)} async-done(((f32[256,256]{1,0:T(8,128)}), f32[4096,256]{1,0:T(8,128)}) %all-gather.19.cloned.1.call-update) | async-done | bytes 4194320 | tf_op jit(solution)/shard_map/all_gather | solution.py:104
  420.7 2.5 reduce_sum.156
  423.2 0.6 select_reduce_fusion.2
  424.5 0.7 multiply_reduce_fusion
  432.1 0.6 fusion.157
  433.3 0.6 constant_dynamic-slice_fusion
  (126 shorter events, 39.8 us)
Async XLA Ops:
  6.5 30.1 %copy-start = (bf16[1024,128]{1,0:T(8,128)(2,1)S(1)}, bf16[1024,128]{1,0:T(8,128)(2,1)}, u32[]{:S(2)}) copy-start(bf16[1024,128]{1,0:T(8,128)(2,1)} %param.10) | copy-start | bytes 786436
  6.5 117.9 %all-gather.11.cloned.1.call-start = ((), (), s32[]{:S(2)}) async-start(), calls=%async_computation | async-start | bytes 4456448 | tf_op jit(solution)/shard_map/all_gather | solution.py:104
  7.5 7.7 %collective-permute-start = (bf16[79,640]{1,0:T(8,128)(2,1)S(1)}, bf16[79,640]{1,0:T(8,128)(2,1)S(1)}, u32[]{:S(2)}, u32[]{:S(2)}) collective-permute-start(bf16[79,640]{1,0:T(8,128)(2,1)S(1)} %slice.51), channel_id=1, source_target_pairs={{0,16},{16,32},{32,48},{48,64},{64,80},{80,96},{96,112},{112,128},... | collective-permute-start | bytes 303368 | tf_op jit(solution)/shard_map/ppermute | solution.py:14
  61.4 7.8 %collective-permute-start.1 = (f32[128,640]{1,0:T(8,128)S(1)}, f32[128,640]{1,0:T(8,128)S(1)}, u32[]{:S(2)}, u32[]{:S(2)}) collective-permute-start(f32[128,640]{1,0:T(8,128)S(1)} %fusion.52), channel_id=1, source_target_pairs={{0,16},{16,0},{32,48},{48,32},{64,80},{80,64},{96,112},{112,96},{1... | collective-permute-start | bytes 983048 | tf_op jit(solution)/shard_map/ppermute | solution.py:20
  70.8 124.3 %all-gather.13.cloned.1.call-start = ((), (), s32[]{:S(2)}) async-start(), calls=%async_computation.1 | async-start | bytes 4456448 | tf_op jit(solution)/shard_map/all_gather | solution.py:104
  133.1 2.7 copy-start.1
  137.0 12.4 %collective-permute-start.2 = (f32[128,640]{1,0:T(8,128)S(1)}, f32[128,640]{1,0:T(8,128)S(1)}, u32[]{:S(2)}, u32[]{:S(2)}) collective-permute-start(f32[128,640]{1,0:T(8,128)S(1)} %fusion.68), channel_id=1, source_target_pairs={{0,32},{16,48},{32,0},{48,16},{64,96},{80,112},{96,64},{112,80},{1... | collective-permute-start | bytes 983048 | tf_op jit(solution)/shard_map/ppermute | solution.py:20
  150.9 113.4 %all-gather.15.cloned.1.call-start = ((), (), s32[]{:S(2)}) async-start(), calls=%async_computation.2 | async-start | bytes 4456448 | tf_op jit(solution)/shard_map/all_gather | solution.py:104
  207.7 10.9 %collective-permute-start.3 = (f32[128,640]{1,0:T(8,128)S(1)}, f32[128,640]{1,0:T(8,128)S(1)}, u32[]{:S(2)}, u32[]{:S(2)}) collective-permute-start(f32[128,640]{1,0:T(8,128)S(1)} %fusion.66), channel_id=1, source_target_pairs={{0,64},{16,80},{32,96},{48,112},{64,0},{80,16},{96,32},{112,48},{1... | collective-permute-start | bytes 983048 | tf_op jit(solution)/shard_map/ppermute | solution.py:20
  220.1 121.3 %all-gather.17.cloned.1.call-start = ((), (), s32[]{:S(2)}) async-start(), calls=%async_computation.3 | async-start | bytes 4456448 | tf_op jit(solution)/shard_map/all_gather | solution.py:104
  276.9 18.8 %collective-permute-start.4 = (f32[128,640]{1,0:T(8,128)S(1)}, f32[128,640]{1,0:T(8,128)S(1)}, u32[]{:S(2)}, u32[]{:S(2)}) collective-permute-start(f32[128,640]{1,0:T(8,128)S(1)} %fusion.64), channel_id=1, source_target_pairs={{0,128},{16,144},{32,160},{48,176},{64,192},{80,208},{96,224},{112... | collective-permute-start | bytes 983048 | tf_op jit(solution)/shard_map/ppermute | solution.py:20
  297.2 123.5 %all-gather.19.cloned.1.call-start = ((), (), s32[]{:S(2)}) async-start(), calls=%async_computation.4 | async-start | bytes 4456448 | tf_op jit(solution)/shard_map/all_gather | solution.py:104
  354.0 18.7 %collective-permute-start.5 = (f32[128,640]{1,0:T(8,128)S(1)}, f32[128,640]{1,0:T(8,128)S(1)}, u32[]{:S(2)}, u32[]{:S(2)}) collective-permute-start(f32[128,640]{1,0:T(8,128)S(1)} %fusion.62), channel_id=1, source_target_pairs={{0,256},{16,272},{32,288},{48,304},{64,320},{80,336},{96,352},{112... | collective-permute-start | bytes 983048 | tf_op jit(solution)/shard_map/ppermute | solution.py:20
Sparse Core Ops, SparseCore 0:
  70.9 53.4 all-gather.10
  151.0 44.0 all-gather.12
  220.2 44.0 all-gather.14
  297.4 44.0 all-gather.16
  374.4 46.3 all-gather.18
